TPU v7x, 256 devices: a whole 4x4x8 slice. The times are simulated.
256 devices in a mesh: fibre: 32 (over x, y, core), group: 8 (over z).
Axes of the slice: x: 4, y: 4, z: 8, core: 2. Of those that a mesh axis runs over, the one named last changes fastest.
Arguments:
- tensor: float32 [512, 393216], P('fibre', 'group'), as said below
Outputs:
- basis: float32 [512, 393216], P('fibre', 'group')
- factor: float32 [512, 512], replicated
Inputs may be any that keep to these rules, and one draw needn't show every extreme that they name: `tensor`: entries are real-valued and the unfolding has full row rank.
All inputs are finite; a program needn't handle non-finite values.
Results may differ from a plain program's by a relative error of at most 0.00018.
Values sent between devices are 32-bit elements; how exact they have to be, the bound alone decides.
A program may use at most 64 MiB of HBM per device.

v0:
```python
import jax
import jax.numpy as jnp
from jax import lax
from jax.sharding import PartitionSpec as P


def partner_2(x, axis, bit):
    return lax.ppermute(x, axis, [(i, i ^ 1 << bit) for i in range(lax.axis_size(axis))])


def local(tensor):
    columns = lax.all_to_all(tensor, "fibre", split_axis=1, concat_axis=0, tiled=True)
    total_cols = columns.shape[1] * lax.axis_size("fibre") * lax.axis_size("group")
    gram = (
        jnp.dot(
            columns, columns.T, precision=lax.Precision.HIGHEST, preferred_element_type=jnp.float32
        )
        / total_cols
    )
    summed = gram
    for bit_number in range(lax.axis_size("fibre").bit_length() - 1):
        partner = partner_2(summed, "fibre", bit_number)
        summed = summed + partner
    for bit_number in range(lax.axis_size("group").bit_length() - 1):
        partner = partner_2(summed, "group", bit_number)
        summed = summed + partner
    factor = jnp.linalg.cholesky(summed)
    solved = lax.linalg.triangular_solve(factor, columns, left_side=True, lower=True)
    basis = lax.all_to_all(solved, "fibre", split_axis=0, concat_axis=1, tiled=True)
    return (basis, factor)


def solution(mesh):
    placed = (P("fibre", "group"),)
    return jax.shard_map(
        local, mesh=mesh, in_specs=placed, out_specs=(P("fibre", "group"), P()), check_vma=False
    )
```

profile of v0, /device:TPU:1, one launch (start us, length us, event | category | flops | bytes accessed | tf_op | source)
XLA Modules:
  0.0 478.2 jit_solution(17674837307822347400)
XLA Ops:
  0.6 2.1 copy.25
  2.7 47.8 %all_to_all.38 = f32[16,32,1536]{2,0,1:T(8,128)S(1)} all-to-all(f32[16,32,1536]{2,0,1:T(8,128)S(1)} %bitcast.70), channel_id=1, replica_groups=mesh['fibre'=32,'group'=8] {'fibre'}, dimensions={1} | all-to-all | bytes 6291456 | tf_op jit(solution)/shard_map/all_to_all | solution.py:12
  50.5 5.1 %convolution_multiply_fusion = f32[512,512]{0,1:T(8,128)S(1)} fusion(f32[512,1536]{1,0:T(8,128)S(1)} %bitcast.66), kind=kOutput, calls=%fused_computation.15 | convolution fusion | flops 4832100352 | bytes 4194304 | tf_op jit(solution)/shard_map/dot_general | solution.py:15
  55.8 2.6 collective-permute-done
  58.7 24.6 %collective-permute-done.1 = f32[512,512]{0,1:T(8,128)S(1)} collective-permute-done((f32[512,512]{0,1:T(8,128)S(1)}, f32[512,512]{0,1:T(8,128)S(1)}, u32[]{:S(2)}, u32[]{:S(2)}) %collective-permute-start.1) | collective-permute-done | bytes 1048608 | tf_op jit(solution)/shard_map/ppermute | solution.py:8
  84.6 24.2 %collective-permute-done.2 = f32[512,512]{0,1:T(8,128)S(1)} collective-permute-done((f32[512,512]{0,1:T(8,128)S(1)}, f32[512,512]{0,1:T(8,128)S(1)}, u32[]{:S(2)}, u32[]{:S(2)}) %collective-permute-start.2) | collective-permute-done | bytes 1048608 | tf_op jit(solution)/shard_map/ppermute | solution.py:8
  109.1 22.9 %collective-permute-done.3 = f32[512,512]{0,1:T(8,128)S(1)} collective-permute-done((f32[512,512]{0,1:T(8,128)S(1)}, f32[512,512]{0,1:T(8,128)S(1)}, u32[]{:S(2)}, u32[]{:S(2)}) %collective-permute-start.3) | collective-permute-done | bytes 1048608 | tf_op jit(solution)/shard_map/ppermute | solution.py:8
  133.5 22.3 %collective-permute-done.4 = f32[512,512]{0,1:T(8,128)S(1)} collective-permute-done((f32[512,512]{0,1:T(8,128)S(1)}, f32[512,512]{0,1:T(8,128)S(1)}, u32[]{:S(2)}, u32[]{:S(2)}) %collective-permute-start.4) | collective-permute-done | bytes 1048608 | tf_op jit(solution)/shard_map/ppermute | solution.py:8
  156.0 1.7 collective-permute-start.5
  157.7 19.9 %collective-permute-done.5 = f32[512,512]{0,1:T(8,128)S(1)} collective-permute-done((f32[512,512]{0,1:T(8,128)S(1)}, f32[512,512]{0,1:T(8,128)S(1)}, u32[]{:S(2)}, u32[]{:S(2)}) %collective-permute-start.5) | collective-permute-done | bytes 1048608 | tf_op jit(solution)/shard_map/ppermute | solution.py:8
  177.8 3.1 collective-permute-start.6
  180.8 44.1 %collective-permute-done.6 = f32[512,512]{0,1:T(8,128)S(1)} collective-permute-done((f32[512,512]{0,1:T(8,128)S(1)}, f32[512,512]{0,1:T(8,128)S(1)}, u32[]{:S(2)}, u32[]{:S(2)}) %collective-permute-start.6) | collective-permute-done | bytes 1048608 | tf_op jit(solution)/shard_map/ppermute | solution.py:8
  226.1 7.1 %collective-permute-start.7 = (f32[512,512]{0,1:T(8,128)}, f32[512,512]{0,1:T(8,128)}, u32[]{:S(2)}, u32[]{:S(2)}) collective-permute-start(f32[512,512]{0,1:T(8,128)} %add.70), channel_id=1, source_target_pairs={{0,4},{1,5},{2,6},{3,7},{4,0},{5,1},{6,2},{7,3},{8,12},{9,13},{10,... | collective-permute-start | bytes 3145736 | tf_op jit(solution)/shard_map/ppermute | solution.py:8
  234.9 43.5 %collective-permute-done.7 = f32[512,512]{0,1:T(8,128)} collective-permute-done((f32[512,512]{0,1:T(8,128)}, f32[512,512]{0,1:T(8,128)}, u32[]{:S(2)}, u32[]{:S(2)}) %collective-permute-start.7) | collective-permute-done | bytes 1048608 | tf_op jit(solution)/shard_map/ppermute | solution.py:8
  278.4 1.7 add.71
  281.7 11.7 %cholesky.104 = f32[128,128]{1,0:T(8,128)S(1)} custom-call(f32[128,128]{1,0:T(8,128)S(1)} %cholesky.266), custom_call_target="Cholesky" | custom-call | tf_op jit(solution)/shard_map/jit(cholesky)/cholesky | solution.py:27
  293.6 9.8 %custom-call.30 = f32[1,128,128]{1,2,0:T(8,128)S(1)} custom-call(f32[1,128,128]{2,1,0:T(8,128)S(1)} %get-tuple-element.35), custom_call_target="InvertDiagBlocksLowerTriangular" | custom-call | tf_op jit(solution)/shard_map/jit(cholesky)/cholesky | solution.py:27
  305.9 11.7 %cholesky.217 = f32[128,128]{1,0:T(8,128)S(1)} custom-call(f32[128,128]{1,0:T(8,128)S(1)} %cholesky.270), custom_call_target="Cholesky" | custom-call | tf_op jit(solution)/shard_map/jit(cholesky)/cholesky | solution.py:27
  317.7 10.0 %custom-call.31 = f32[1,128,128]{1,2,0:T(8,128)S(1)} custom-call(f32[1,128,128]{2,1,0:T(8,128)S(1)} %get-tuple-element.32), custom_call_target="InvertDiagBlocksLowerTriangular" | custom-call | tf_op jit(solution)/shard_map/jit(cholesky)/cholesky | solution.py:27
  329.2 11.7 %cholesky.238 = f32[128,128]{1,0:T(8,128)S(1)} custom-call(f32[128,128]{1,0:T(8,128)S(1)} %cholesky.275), custom_call_target="Cholesky" | custom-call | tf_op jit(solution)/shard_map/jit(cholesky)/cholesky | solution.py:27
  341.0 9.8 %custom-call.32 = f32[1,128,128]{1,2,0:T(8,128)S(1)} custom-call(f32[1,128,128]{2,1,0:T(8,128)S(1)} %get-tuple-element.29), custom_call_target="InvertDiagBlocksLowerTriangular" | custom-call | tf_op jit(solution)/shard_map/jit(cholesky)/cholesky | solution.py:27
  352.3 11.9 %cholesky.255 = f32[128,128]{1,0:T(8,128)S(1)} custom-call(f32[128,128]{1,0:T(8,128)S(1)} %slice_subtract_fusion.2), custom_call_target="Cholesky" | custom-call | tf_op jit(solution)/shard_map/jit(cholesky)/cholesky | solution.py:27
  370.4 11.7 %while.1 = (s32[]{:T(128)}, f32[512,512]{1,0:T(8,128)}, s32[4,2]{0,1:T(2,128)S(1)}, f32[4,128,128]{2,1,0:T(8,128)S(1)}, s32[]{:T(128)}) while((s32[]{:T(128)}, f32[512,512]{1,0:T(8,128)}, s32[4,2]{0,1:T(2,128)S(1)}, f32[4,128,128]{2,1,0:T(8,128)S(1)}, s32[]{:T(128)}) %tuple.35), condition=%wide.while_cond, body=%wide.while_body.sunk | while | flops 2 | bytes 131189 | solution.py:28
  371.1 2.2 bitcast_dynamic-update-slice_fusion.2
  374.0 2.2 bitcast_dynamic-update-slice_fusion.2
  376.9 2.2 bitcast_dynamic-update-slice_fusion.2
  379.9 2.2 bitcast_dynamic-update-slice_fusion.2
  382.1 39.3 %custom-call.33 = f32[4,128,128]{1,2,0:T(8,128)S(1)} custom-call(f32[4,128,128]{2,1,0:T(8,128)S(1)} %get-tuple-element.9), custom_call_target="InvertDiagBlocksLowerTriangular" | custom-call | tf_op jit(solution)/shard_map/triangular_solve | solution.py:28
  424.8 1.9 convolution_subtract_fusion
  427.5 2.5 convolution_subtract_fusion.1
  431.1 44.8 %all_to_all.39 = f32[32,16,1536]{2,1,0:T(8,128)S(1)} all-to-all(f32[32,16,1536]{2,1,0:T(8,128)S(1)} %bitcast.68), channel_id=1, replica_groups=mesh['fibre'=32,'group'=8] {'fibre'}, dimensions={0} | all-to-all | bytes 6291456 | tf_op jit(solution)/shard_map/all_to_all | solution.py:29
  475.9 1.9 copy.23
  (60 shorter events, 25.7 us)
Async XLA Ops:
  55.6 2.7 collective-permute-start
  58.6 24.7 %collective-permute-start.1 = (f32[512,512]{0,1:T(8,128)S(1)}, f32[512,512]{0,1:T(8,128)S(1)}, u32[]{:S(2)}, u32[]{:S(2)}) collective-permute-start(f32[512,512]{0,1:T(8,128)S(1)} %add.64), channel_id=1, source_target_pairs={{0,16},{8,24},{16,0},{24,8},{32,48},{40,56},{48,32},{56,40},{64,80... | collective-permute-start | bytes 3145736 | tf_op jit(solution)/shard_map/ppermute | solution.py:8
  83.5 25.3 %collective-permute-start.2 = (f32[512,512]{0,1:T(8,128)S(1)}, f32[512,512]{0,1:T(8,128)S(1)}, u32[]{:S(2)}, u32[]{:S(2)}) collective-permute-start(f32[512,512]{0,1:T(8,128)S(1)} %add.65), channel_id=1, source_target_pairs={{0,32},{8,40},{16,48},{24,56},{32,0},{40,8},{48,16},{56,24},{64,96... | collective-permute-start | bytes 3145736 | tf_op jit(solution)/shard_map/ppermute | solution.py:8
  109.0 23.0 %collective-permute-start.3 = (f32[512,512]{0,1:T(8,128)S(1)}, f32[512,512]{0,1:T(8,128)S(1)}, u32[]{:S(2)}, u32[]{:S(2)}) collective-permute-start(f32[512,512]{0,1:T(8,128)S(1)} %add.66), channel_id=1, source_target_pairs={{0,64},{8,72},{16,80},{24,88},{32,96},{40,104},{48,112},{56,120},{... | collective-permute-start | bytes 3145736 | tf_op jit(solution)/shard_map/ppermute | solution.py:8
  132.1 23.6 %collective-permute-start.4 = (f32[512,512]{0,1:T(8,128)S(1)}, f32[512,512]{0,1:T(8,128)S(1)}, u32[]{:S(2)}, u32[]{:S(2)}) collective-permute-start(f32[512,512]{0,1:T(8,128)S(1)} %add.67), channel_id=1, source_target_pairs={{0,128},{8,136},{16,144},{24,152},{32,160},{40,168},{48,176},{56,1... | collective-permute-start | bytes 3145736 | tf_op jit(solution)/shard_map/ppermute | solution.py:8
  156.0 21.6 %collective-permute-start.5 = (f32[512,512]{0,1:T(8,128)S(1)}, f32[512,512]{0,1:T(8,128)S(1)}, u32[]{:S(2)}, u32[]{:S(2)}) collective-permute-start(f32[512,512]{0,1:T(8,128)S(1)} %add.68), channel_id=1, source_target_pairs={{0,1},{1,0},{2,3},{3,2},{4,5},{5,4},{6,7},{7,6},{8,9},{9,8},{10,11... | collective-permute-start | bytes 3145736 | tf_op jit(solution)/shard_map/ppermute | solution.py:8
  177.8 47.1 %collective-permute-start.6 = (f32[512,512]{0,1:T(8,128)S(1)}, f32[512,512]{0,1:T(8,128)S(1)}, u32[]{:S(2)}, u32[]{:S(2)}) collective-permute-start(f32[512,512]{0,1:T(8,128)S(1)} %add.69), channel_id=1, source_target_pairs={{0,2},{1,3},{2,0},{3,1},{4,6},{5,7},{6,4},{7,5},{8,10},{9,11},{10,... | collective-permute-start | bytes 3145736 | tf_op jit(solution)/shard_map/ppermute | solution.py:8
  226.1 52.3 %collective-permute-start.7 = (f32[512,512]{0,1:T(8,128)}, f32[512,512]{0,1:T(8,128)}, u32[]{:S(2)}, u32[]{:S(2)}) collective-permute-start(f32[512,512]{0,1:T(8,128)} %add.70), channel_id=1, source_target_pairs={{0,4},{1,5},{2,6},{3,7},{4,0},{5,1},{6,2},{7,3},{8,12},{9,13},{10,... | collective-permute-start | bytes 3145736 | tf_op jit(solution)/shard_map/ppermute | solution.py:8
  280.7 1.0 copy-start.4
  305.9 115.5 %copy-start = (f32[8,16,1536]{2,1,0:T(8,128)S(1)}, f32[8,16,1536]{2,1,0:T(8,128)}, u32[]{:S(2)}) copy-start(f32[8,16,1536]{2,1,0:T(8,128)} %get-tuple-element.22) | copy-start | bytes 2359300
  350.8 71.5 %copy-start.2 = (f32[8,16,1536]{2,1,0:T(8,128)S(1)}, f32[8,16,1536]{2,1,0:T(8,128)}, u32[]{:S(2)}) copy-start(f32[8,16,1536]{2,1,0:T(8,128)} %get-tuple-element.24) | copy-start | bytes 2359300
  370.4 54.4 %copy-start.1 = (f32[8,16,1536]{2,1,0:T(8,128)S(1)}, f32[8,16,1536]{2,1,0:T(8,128)}, u32[]{:S(2)}) copy-start(f32[8,16,1536]{2,1,0:T(8,128)} %get-tuple-element.23) | copy-start | bytes 2359300
  423.9 3.6 copy-start.3
where the time goes:
time: 487 us; the launch traced here: 478 us
  waiting for transfers between devices  204 us (42%)
  other arithmetic  124 us (25%)
  blocking collectives  92.6 us (19%)
  matrix products  20 us (4%)
  local copies, waits for them, and re-layouts  18.7 us (4%)
  starting transfers between devices  14.7 us (3%)
    ppermute x8, waiting for transfers between devices, partner_2(): lax.ppermute(x, axis, [(i, i ^ 1 << bit) for i in range(lax.axis_size(axi...  204 us
    another operation x14, other arithmetic, local(): factor = jnp.linalg.cholesky(summed)  78.8 us
    all_to_all x1, blocking collectives, local(): lax.all_to_all(tensor, 'fibre', split_axis=1, concat_axis=0, tiled=True)  47.8 us
    all_to_all x1, blocking collectives, local(): lax.all_to_all(solved, 'fibre', split_axis=0, concat_axis=1, tiled=True)  44.8 us
    another operation x4, other arithmetic, local(): lax.linalg.triangular_solve(factor, columns, left_side=True, lower=True)  41.1 us
    ppermute x8, starting transfers between devices, partner_2(): lax.ppermute(x, axis, [(i, i ^ 1 << bit) for i in range(lax.axis_size(axi...  14.7 us
    another operation x12, local copies, waits for them, and re-layouts  11.6 us
  transfers between devices with their start and end apart: 8, of which 8 were waited for; matrix products, arithmetic and copies ran while one was open for 0% of the time, Pallas kernels for 0%

commit v1 on v0

v1 whole, which is shorter than its diff:
```python
import jax
import jax.numpy as jnp
from jax import lax
from jax.experimental import pallas as pl
from jax.experimental.pallas import tpu as pltpu
from jax.sharding import PartitionSpec as P

HI = lax.Precision.HIGHEST
MESH = pl.DeviceIdType.MESH
M = 512
NF = 32
NG = 8
W = 1536
COLS = W * NF * NG
PACK = 1280
OWN = PACK // NF
FAR = sorted(
    [(dx, dy, dc) for dx in range(4) for dy in range(4) for dc in range(2) if (dx, dy, dc) != (0, 0, 0)],
    key=lambda t: -(min(t[0], 4 - t[0]) + min(t[1], 4 - t[1])),
)


def peer(me, t):
    x, y, c = me // 8, (me // 2) % 4, me % 2
    return ((x + t[0]) % 4 * 4 + (y + t[1]) % 4) * 2 + (c + t[2]) % 2


def rows(i, n):
    return pl.ds(pl.multiple_of(i * n, 8), n)


def lanes(i, n):
    return pl.ds(pl.multiple_of(i * n, 128), n)


def bdot(a, b, ca, cb):
    return lax.dot_general(a, b, (((ca,), (cb,)), ((), ())), preferred_element_type=jnp.float32)


def gather_gram(x_ref, hi_ref, lo_ref, g_ref, cols, part, parts, mine, planes, s0, r0, s1, r1, s2, r2, s3, r3, ls):
    me, g = lax.axis_index("fibre"), lax.axis_index("group")
    bar = pltpu.get_barrier_semaphore()
    for t in FAR:
        pl.semaphore_signal(bar, inc=1, device_id=(peer(me, t), g), device_id_type=MESH)
    for k in range(1, NG):
        pl.semaphore_signal(bar, inc=1, device_id=(me, (g + k) % NG), device_id_type=MESH)
    pl.semaphore_wait(bar, NF + NG - 2)

    def send(src, dst, to, s, r, i):
        c = pltpu.make_async_remote_copy(
            src_ref=src, dst_ref=dst, send_sem=s.at[i], recv_sem=r.at[i], device_id=to, device_id_type=MESH
        )
        c.start()
        return c

    cs = [
        send(x_ref.at[:, lanes(peer(me, t), W)], cols.at[rows(me, 16), :], (peer(me, t), g), s0, r0, i)
        for i, t in enumerate(FAR)
    ]
    own = pltpu.make_async_copy(x_ref.at[:, lanes(me, W)], cols.at[rows(me, 16), :], ls)
    own.start()
    for c in cs:
        c.wait()
    own.wait()

    for k in range(4):
        v = cols[128 * k : 128 * k + 128, :]
        top = v.astype(jnp.bfloat16)
        hi_ref[128 * k : 128 * k + 128, :] = top
        lo_ref[128 * k : 128 * k + 128, :] = (v - top.astype(jnp.float32)).astype(jnp.bfloat16)
    for i in range(4):
        a, al = hi_ref[128 * i : 128 * i + 128, :], lo_ref[128 * i : 128 * i + 128, :]
        n = 128 * (i + 1)
        b, bl = hi_ref[0:n, :], lo_ref[0:n, :]
        blk = (bdot(a, b, 1, 1) + (bdot(a, bl, 1, 1) + bdot(al, b, 1, 1))) * (1.0 / COLS)
        for j in range(i + 1):
            o = 128 * (i * (i + 1) // 2 + j)
            part[o : o + 128, :] = blk[:, 128 * j : 128 * j + 128]

    cs = [
        send(part.at[rows(peer(me, t), OWN), :], parts.at[me], (peer(me, t), g), s1, r1, i) for i, t in enumerate(FAR)
    ]
    parts[me] = part[rows(me, OWN), :]
    for c in cs:
        c.wait()
    mine[...] = parts[0]
    for f in range(1, NF):
        mine[...] += parts[f]

    cs = [
        send(mine, planes.at[g], (me, (g + k) % NG), s2, r2, k - 1) for k in range(1, NG)
    ]
    planes[g] = mine[...]
    for c in cs:
        c.wait()
    total = planes[0]
    for f in range(1, NG):
        total = total + planes[f]
    g_ref[rows(me, OWN), :] = total

    cs = [
        send(g_ref.at[rows(me, OWN), :], g_ref.at[rows(me, OWN), :], (peer(me, t), g), s3, r3, i)
        for i, t in enumerate(FAR)
    ]
    for c in cs:
        c.wait()


def dot(a,b,ca=1,cb=0):
    return lax.dot_general(a,b,(((ca,),(cb,)),((),())),precision=HI,preferred_element_type=jnp.float32)
def diag_block(w):
    lane=lax.broadcasted_iota(jnp.int32,(8,128),1)
    sub=lax.broadcasted_iota(jnp.int32,(8,128),0)
    gather=lambda v,j:jnp.take_along_axis(v,jnp.full((8,128),j,jnp.int32),axis=1)
    spread=lambda v,r:jnp.broadcast_to(v[r:r+1,:],(8,128))
    def apply(A,W,base):
        group=(lane>=base)&(lane<base+8)
        t=[gather(A,base+r)*W[r] for r in range(8)]
        return jnp.where(group,0.0,A)-(((t[0]+t[1])+(t[2]+t[3]))+((t[4]+t[5])+(t[6]+t[7])))
    def step(p,carry):
        R,Wp=carry
        base=pl.multiple_of(8*p,8)
        kept=R
        B=[gather(R,base+c) for c in range(8)]
        for r in range(8):
            hit=lane==base+r
            row=spread(R,r)
            kept=jnp.where(sub==r,row,kept)
            inv=1.0/spread(B[r],r)
            m=B[r]*inv
            for c in range(r+1,8):
                rc=spread(B[c],r)
                B[c]=jnp.where(sub==r,rc*inv,B[c]-m*rc)
            R=jnp.where(sub==r,jnp.where(hit,1.0,row)*inv,jnp.where(hit,0.0,R)-m*jnp.where(hit,1.0,row))
        prev=jnp.maximum(base-8,0)
        Wl=[spread(Wp,r) for r in range(8)]
        for i in range(2,16):
            A=w[8*i:8*i+8,:]
            w[8*i:8*i+8,:]=jnp.where(i>p,jnp.where(p>0,apply(A,Wl,prev),A),A)
        w[pl.ds(base,8),:]=kept
        W=[spread(R,r) for r in range(8)]
        nxt=apply(w[pl.ds(base+8,8),:],W,base)
        return nxt,R
    lax.fori_loop(0,16,step,(w[0:8,:],jnp.zeros((8,128),jnp.float32)))
def chol_kernel(g_ref, l_ref, hi_ref, lo_ref, a_ref, li_ref, w):
    B=128; nb=4
    l_ref[...]=jnp.zeros((512,512),jnp.float32)
    li_ref[...]=jnp.zeros((512,512),jnp.float32)
    for i in range(4):
        for j in range(i+1):
            b = i*(i+1)//2+j
            a_ref[128*i:128*i+128,128*j:128*j+128]=g_ref[128*b:128*b+128,:]
    ri=lax.broadcasted_iota(jnp.int32,(B,B),0); ci=lax.broadcasted_iota(jnp.int32,(B,B),1)
    for k in range(nb):
        o=k*B; n=512-o-B
        w[0:B,:]=a_ref[o:o+B,o:o+B]
        diag_block(w)
        A=w[0:B,:]
        d=jnp.sum(jnp.where(ri==ci,A,0.0),axis=1,keepdims=True)
        rs=lax.rsqrt(d)
        U=jnp.where(ci>=ri,A,0.0)*rs
        LI=jnp.where(ci<ri,A,jnp.where(ri==ci,1.0,0.0))*rs
        l_ref[o:o+B,o:o+B]=U.T
        if n:
            L21=dot(a_ref[o+B:,o:o+B],LI,1,1)
            l_ref[o+B:,o:o+B]=L21
            a_ref[o+B:,o+B:]=a_ref[o+B:,o+B:]-dot(L21,L21,1,1)
        if k:
            T=dot(l_ref[o:o+B,0:o],li_ref[0:o,0:o])
            li_ref[o:o+B,0:o]=-dot(LI,T)
        li_ref[o:o+B,o:o+B]=LI
    li = li_ref[...]
    top = li.astype(jnp.bfloat16)
    hi_ref[...] = top
    lo_ref[...] = (li - top.astype(jnp.float32)).astype(jnp.bfloat16)


def solve_scatter(hi_ref, lo_ref, lh_ref, ll_ref, o_ref, buf, s, r, ls):
    me, g = lax.axis_index("fibre"), lax.axis_index("group")
    bar = pltpu.get_barrier_semaphore()
    for t in FAR:
        pl.semaphore_signal(bar, inc=1, device_id=(peer(me, t), g), device_id_type=MESH)
    cs = []
    for n, dx in enumerate((2, 1, 3, 0)):
        k = (me // 8 + dx) % 4
        lh, ll = lh_ref[rows(k, 128), :], ll_ref[rows(k, 128), :]
        hi = hi_ref[...]
        buf[rows(k, 128), :] = bdot(lh, hi, 1, 0) + (bdot(lh, lo_ref[...], 1, 0) + bdot(ll, hi, 1, 0))
        if n == 0:
            pl.semaphore_wait(bar, NF - 1)
        for i, t in enumerate(FAR):
            if t[0] == dx:
                p = peer(me, t)
                c = pltpu.make_async_remote_copy(
                    src_ref=buf.at[rows(p, 16), :],
                    dst_ref=o_ref.at[:, lanes(me, W)],
                    send_sem=s.at[i],
                    recv_sem=r.at[i],
                    device_id=(p, g),
                    device_id_type=MESH,
                )
                c.start()
                cs.append(c)
    own = pltpu.make_async_copy(buf.at[rows(me, 16), :], o_ref.at[:, lanes(me, W)], ls)
    own.start()
    for c in cs:
        c.wait()
    own.wait()


def local(tensor):
    f32, bf16, shape = jnp.float32, jnp.bfloat16, jax.ShapeDtypeStruct
    vmem, dma = pl.BlockSpec(memory_space=pltpu.VMEM), pltpu.SemaphoreType.DMA
    hi, lo, gram = pl.pallas_call(
        gather_gram,
        out_shape=(shape((M, W), bf16), shape((M, W), bf16), shape((PACK, 128), f32)),
        in_specs=[pl.BlockSpec(memory_space=pl.ANY)],
        out_specs=(vmem, vmem, vmem),
        scratch_shapes=[
            pltpu.VMEM((M, W), f32),
            pltpu.VMEM((PACK, 128), f32),
            pltpu.VMEM((NF, OWN, 128), f32),
            pltpu.VMEM((OWN, 128), f32),
            pltpu.VMEM((NG, OWN, 128), f32),
            dma((NF - 1,)),
            dma((NF - 1,)),
            dma((NF - 1,)),
            dma((NF - 1,)),
            dma((NG - 1,)),
            dma((NG - 1,)),
            dma((NF - 1,)),
            dma((NF - 1,)),
            dma,
        ],
        compiler_params=pltpu.CompilerParams(collective_id=0, has_side_effects=True, vmem_limit_bytes=32 << 20),
    )(tensor)
    factor, lh, ll = pl.pallas_call(
        chol_kernel,
        out_shape=(shape((M, M), f32), shape((M, M), bf16), shape((M, M), bf16)),
        in_specs=[vmem],
        out_specs=(vmem, vmem, vmem),
        scratch_shapes=[pltpu.VMEM((M, M), f32), pltpu.VMEM((M, M), f32), pltpu.VMEM((136, 128), f32)],
        compiler_params=pltpu.CompilerParams(vmem_limit_bytes=32 << 20),
    )(gram)
    basis = pl.pallas_call(
        solve_scatter,
        out_shape=shape(tensor.shape, f32),
        in_specs=[vmem] * 4,
        out_specs=pl.BlockSpec(memory_space=pl.ANY),
        scratch_shapes=[pltpu.VMEM((M, W), f32), dma((NF - 1,)), dma((NF - 1,)), dma],
        compiler_params=pltpu.CompilerParams(collective_id=1, has_side_effects=True, vmem_limit_bytes=32 << 20),
    )(hi, lo, lh, ll)
    return basis, factor


def solution(mesh):
    return jax.shard_map(
        local,
        mesh=mesh,
        in_specs=(P("fibre", "group"),),
        out_specs=(P("fibre", "group"), P()),
        check_vma=False,
    )
```

time: 487 us -> 176 us (0.36); the launches traced: 478 us -> 175 us
  waiting for transfers between devices: 204 us -> 0 us
  Pallas kernels: 0 us -> 171 us
  other arithmetic: 124 us -> 0 us
  blocking collectives: 92.6 us -> 0 us
  matrix products: 20 us -> 0 us
  local copies, waits for them, and re-layouts: 18.7 us -> 3.55 us
  starting transfers between devices: 14.7 us -> 0 us
    ppermute x8 -> x0, waiting for transfers between devices: 204 us -> none  [partner_2(): lax.ppermute(x, axis, [(i, i ^ 1 << bit) for i in range(lax.axis_size(axi...]
    pallas_call x0 -> x3, Pallas kernels: none -> 171 us  [the longest x1 85.6 us: local(): pl.pallas_call(gather_gram, out_shape=(shape((M, W), bf16), shape((M, W),...]
    another operation x18 -> x0, other arithmetic: 120 us -> none  [the longest x14 78.8 us: local(): factor = jnp.linalg.cholesky(summed)]
    all_to_all x2 -> x0, blocking collectives: 92.6 us -> none  [the longest x1 47.8 us: local(): lax.all_to_all(tensor, 'fibre', split_axis=1, concat_axis=0, tiled=True)]
    another operation x13 -> x0, matrix products: 14.9 us -> none  [the longest x7 9.39 us: local(): lax.linalg.triangular_solve(factor, columns, left_side=True, lower=True)]
    ppermute x8 -> x0, starting transfers between devices: 14.7 us -> none  [partner_2(): lax.ppermute(x, axis, [(i, i ^ 1 << bit) for i in range(lax.axis_size(axi...]
    another operation x18 -> x0, local copies, waits for them, and re-layouts: 13.5 us -> none
    dot_general x1 -> x0, matrix products: 5.12 us -> none  [local(): jnp.dot(columns, columns.T, precision=lax.Precision.HIGHEST, preferred_el...]
  transfers between devices with their start and end apart: 8 -> 0, of which waited for: 8 -> 0; matrix products, arithmetic and copies ran while one was open for 0% -> 0% of each run, Pallas kernels for 0% -> 0%
where the time goes in v1:
time: 176 us; the launch traced here: 175 us
  Pallas kernels  171 us (97%)
  local copies, waits for them, and re-layouts  3.55 us (2%)
    pallas_call x1, Pallas kernels, local(): pl.pallas_call(gather_gram, out_shape=(shape((M, W), bf16), shape((M, W),...  85.6 us
    pallas_call x1, Pallas kernels, local(): pl.pallas_call(solve_scatter, out_shape=shape(tensor.shape, f32), in_spec...  48.2 us
    pallas_call x1, Pallas kernels, local(): pl.pallas_call(chol_kernel, out_shape=(shape((M, M), f32), shape((M, M),...  37.4 us
    unnamed x3, local copies, waits for them, and re-layouts  3.55 us

profile of v1, /device:TPU:1, one launch (start us, length us, event | category | flops | bytes accessed | tf_op | source)
XLA Modules:
  0.0 175.4 jit_solution(8207470644769124502)
XLA Ops:
  0.6 0.0 copy-start
  0.6 1.9 %copy-done = f32[16,49152]{1,0:T(8,128)S(1)} copy-done((f32[16,49152]{1,0:T(8,128)S(1)}, f32[16,49152]{1,0:T(8,128)}, u32[]{:S(2)}) %copy-start) | copy-done | bytes 3145752
  2.5 85.6 %shard_map.30 = (bf16[512,1536]{1,0:T(8,128)(2,1)S(1)}, bf16[512,1536]{1,0:T(8,128)(2,1)S(1)}, f32[1280,128]{1,0:T(8,128)S(1)}) custom-call(f32[16,49152]{1,0:T(8,128)S(1)} %copy-done), custom_call_target="tpu_custom_call" | custom-call | tf_op jit(solution)/shard_map/pallas_call | solution.py:214
  88.1 37.4 %shard_map.31 = (f32[512,512]{1,0:T(8,128)}, bf16[512,512]{1,0:T(8,128)(2,1)S(1)}, bf16[512,512]{1,0:T(8,128)(2,1)S(1)}) custom-call(f32[1280,128]{1,0:T(8,128)S(1)} %get-tuple-element.10.g_ref), custom_call_target="tpu_custom_call" | custom-call | tf_op jit(solution)/shard_map/pallas_call | solution.py:237
  125.5 48.2 %shard_map.32 = f32[16,49152]{1,0:T(8,128)S(1)} custom-call(bf16[512,1536]{1,0:T(8,128)(2,1)S(1)} %get-tuple-element.8.hi_ref, bf16[512,1536]{1,0:T(8,128)(2,1)S(1)} %get-tuple-element.9.lo_ref, bf16[512,512]{1,0:T(8,128)(2,1)S(1)} %get-tuple-element.11.lh_ref, bf16[512,512]{1,0:T(8,128)(2,1)S(1)} %get-tuple-element.12.ll_ref), custom_call_target="tpu_custom_call" | custom-call | tf_op jit(solution)/shard_map/pallas_call | solution.py:245
  173.8 1.7 copy.4
Async XLA Ops:
  0.6 1.9 %copy-start = (f32[16,49152]{1,0:T(8,128)S(1)}, f32[16,49152]{1,0:T(8,128)}, u32[]{:S(2)}) copy-start(f32[16,49152]{1,0:T(8,128)} %x_ref.1) | copy-start | bytes 9437188

commit v2 on v0

v2 whole, which is shorter than its diff:
```python
import jax
import jax.numpy as jnp
from jax import lax
from jax.experimental import pallas as pl
from jax.experimental.pallas import tpu as pltpu
from jax.sharding import PartitionSpec as P

HI = lax.Precision.HIGHEST
MESH = pl.DeviceIdType.MESH
M = 512
NF = 32
NG = 8
W = 1536
COLS = W * NF * NG
PACK = 1280
OWN = PACK // NF
HALF = PACK // 2
CHUNKS = ((0, 24), (24, 16))
CHIPS = sorted(
    [(dx, dy) for dx in range(4) for dy in range(4) if (dx, dy) != (0, 0)],
    key=lambda t: -(min(t[0], 4 - t[0]) + min(t[1], 4 - t[1])),
)
FAR = sorted(
    [(dx, dy, dc) for dx in range(4) for dy in range(4) for dc in range(2) if (dx, dy, dc) != (0, 0, 0)],
    key=lambda t: -(min(t[0], 4 - t[0]) + min(t[1], 4 - t[1])),
)


def peer(me, t):
    x, y, c = me // 8, (me // 2) % 4, me % 2
    return ((x + t[0]) % 4 * 4 + (y + t[1]) % 4) * 2 + (c + t[2]) % 2


def chip(x, y, c):
    return ((x % 4) * 4 + y % 4) * 2 + c % 2


def exchange(pair, one, slot, slot_one, dst, sems, local_sem, order=(2, 1, 3), hook=None):
    s1, r1, s2, r2 = sems
    me, g = lax.axis_index("fibre"), lax.axis_index("group")
    x, y, c = me // 8, (me // 2) % 4, me % 2
    first, last, own = {}, [], []

    def go(h, d, e, dc, src, f):
        to = chip(x, y + e, c + dc) if h == 0 else chip(x + e, y, c + dc)
        if e == 0 and dc == 0:
            k = pltpu.make_async_copy(src, dst(h, f), local_sem.at[h, d])
            own.append(k)
        else:
            k = pltpu.make_async_remote_copy(
                src_ref=src, dst_ref=dst(h, f), send_sem=s2.at[h, d, e, dc], recv_sem=r2.at[h, d, e, dc],
                device_id=(to, g), device_id_type=MESH,
            )
            last.append(k)
        k.start()

    for h, d, e in (
        [(h, d, e) for d in order for e in (2, 1, 3, 0) for h in range(2)]
        if hook is None
        else [(h, d, e) for h in range(2) for d in order for e in (2, 1, 3, 0)]
    ):
                if hook is not None and (d, e) == (order[0], 2):
                    hook(h)
                X, Y = (x + d, y + e) if h == 0 else (x + e, y + d)
                to = chip(x + d, y, c) if h == 0 else chip(x, y + d, c)
                k = pltpu.make_async_remote_copy(
                    src_ref=pair(h, X % 4, Y % 4), dst_ref=slot(h, d, e), send_sem=s1.at[h, d, e],
                    recv_sem=r1.at[h, d, e], device_id=(to, g), device_id_type=MESH,
                )
                k.start()
                first[h, d, e] = k
    for e in (2, 1, 3, 0):
        for dc in range(2):
            for h in range(2):
                X, Y = (x, y + e) if h == 0 else (x + e, y)
                go(h, 0, e, dc, one(h, X % 4, Y % 4, (c + dc) % 2), me)
    for d in order:
        for e in (2, 1, 3, 0):
            for h in range(2):
                first[h, d, e].wait_recv()
                f = chip(x - d + 4, y, c) if h == 0 else chip(x, y - d + 4, c)
                for dc in range(2):
                    go(h, d, e, dc, slot_one(h, d, e, (c + dc) % 2), f)
    for k in first.values():
        k.wait_send()
    for k in last + own:
        k.wait()


def cross(me):
    x, y, c = me // 8, (me // 2) % 4, me % 2
    t = [(0, 0, 1)] + [(d, 0, k) for d in (1, 2, 3) for k in (0, 1)] + [(0, d, k) for d in (1, 2, 3) for k in (0, 1)]
    return [chip(x + a, y + b, c + k) for a, b, k in t]


def rows(i, n):
    return pl.ds(pl.multiple_of(i * n, 8), n)


def lanes(i, n):
    return pl.ds(pl.multiple_of(i * n, 128), n)


def bdot(a, b, ca, cb):
    return lax.dot_general(a, b, (((ca,), (cb,)), ((), ())), preferred_element_type=jnp.float32)


def gather_gram(x_ref, hi_ref, lo_ref, g_ref, cols, relay, part, pair, keep, parts, mine, planes, sa, ra, sb, rb, ls,
                s0, r0, s1, r1, s2, r2, s3, r3, s4, r4):
    me, g = lax.axis_index("fibre"), lax.axis_index("group")
    bar = pltpu.get_barrier_semaphore()
    for t in FAR:
        pl.semaphore_signal(bar, inc=1, device_id=(peer(me, t), g), device_id_type=MESH)
    for k in range(1, NG):
        pl.semaphore_signal(bar, inc=1, device_id=(me, (g + k) % NG), device_id_type=MESH)
    pl.semaphore_wait(bar, NF + NG - 2)

    def send(src, dst, to, s, r, i):
        c = pltpu.make_async_remote_copy(
            src_ref=src, dst_ref=dst, send_sem=s.at[i], recv_sem=r.at[i], device_id=to, device_id_type=MESH
        )
        c.start()
        return c

    exchange(
        lambda h, X, Y: x_ref.at[8 * h : 8 * h + 8, lanes(X * 4 + Y, 2 * W)],
        lambda h, X, Y, C: x_ref.at[8 * h : 8 * h + 8, lanes((X * 4 + Y) * 2 + C, W)],
        lambda h, d, e: relay.at[h, d - 1, e],
        lambda h, d, e, C: relay.at[h, d - 1, e, :, lanes(C, W)],
        lambda h, f: cols.at[rows(2 * f + h, 8), :],
        (sa, ra, sb, rb),
        ls,
    )

    for k in range(4):
        v = cols[128 * k : 128 * k + 128, :]
        top = v.astype(jnp.bfloat16)
        hi_ref[128 * k : 128 * k + 128, :] = top
        lo_ref[128 * k : 128 * k + 128, :] = (v - top.astype(jnp.float32)).astype(jnp.bfloat16)
    for i in range(4):
        a, al = hi_ref[128 * i : 128 * i + 128, :], lo_ref[128 * i : 128 * i + 128, :]
        n = 128 * (i + 1)
        b, bl = hi_ref[0:n, :], lo_ref[0:n, :]
        blk = (bdot(a, b, 1, 1) + (bdot(a, bl, 1, 1) + bdot(al, b, 1, 1))) * (1.0 / COLS)
        for j in range(i + 1):
            o = 128 * (i * (i + 1) // 2 + j)
            part[o : o + 128, :] = blk[:, 128 * j : 128 * j + 128]

    x, y, c = me // 8, (me // 2) % 4, me % 2
    p, twin = me // 2, (chip(x, y, c + 1), g)
    ks = range(len(CHUNKS))

    def span(core, k):
        return pl.ds(pl.multiple_of(core * HALF + 16 * CHUNKS[k][0], 8), 16 * CHUNKS[k][1])

    def piece(core, k, q):
        return pl.ds(pl.multiple_of(core * HALF + 16 * CHUNKS[k][0] + q * CHUNKS[k][1], 8), CHUNKS[k][1])

    def near(k):
        return pl.ds(16 * CHUNKS[k][0], 16 * CHUNKS[k][1])

    swap = [send(part.at[span(1 - c, k), :], pair.at[near(k), :], twin, s0, r0, k) for k in ks]
    plane = []
    for k in ks:
        swap[k].wait_recv()
        keep[near(k), :] = part[span(c, k), :] + pair[near(k), :]
        o, n = CHUNKS[k]
        cs = []
        for i, t in enumerate(CHIPS):
            q = chip(x + t[0], y + t[1], c)
            src = keep.at[pl.ds(pl.multiple_of(16 * o + (q // 2) * n, 8), n), :]
            cs.append(send(src, parts.at[p, o : o + n, :], (q, g), s1, r1, 15 * k + i))
        parts[p, o : o + n, :] = keep[pl.ds(pl.multiple_of(16 * o + p * n, 8), n), :]
        plane.append(cs)

    def added(ref, count, o, n):
        v = [ref[f, o : o + n, :] for f in range(count)]
        while len(v) > 1:
            v = [v[f] + v[f + 1] for f in range(0, len(v), 2)]
        return v[0]

    depth = []
    for k in ks:
        o, n = CHUNKS[k]
        for q in plane[k]:
            q.wait_recv()
        mine[o : o + n, :] = added(parts, NF // 2, o, n)
        depth.append([
            send(mine.at[o : o + n, :], planes.at[g, o : o + n, :], (me, (g + d) % NG), s2, r2, 7 * k + d - 1)
            for d in (4, 3, 5, 2, 6, 1, 7)
        ])
        planes[g, o : o + n, :] = mine[o : o + n, :]

    spread, over = [], []
    for k in ks:
        o, n = CHUNKS[k]
        for q in depth[k]:
            q.wait_recv()
        g_ref[piece(c, k, p), :] = added(planes, NG, o, n)
        own = g_ref.at[piece(c, k, p), :]
        spread.append([
            send(own, own, (chip(x + t[0], y + t[1], c), g), s3, r3, 15 * k + i) for i, t in enumerate(CHIPS)
        ])
        over.append(send(own, own, twin, s4, r4, 16 * k + 15))
    for k in ks:
        for i in reversed(range(15)):
            t = CHIPS[i]
            spread[k][i].wait_recv()
            got = g_ref.at[piece(c, k, chip(x - t[0] + 4, y - t[1] + 4, 0) // 2), :]
            over.append(send(got, got, twin, s4, r4, 16 * k + i))
    for q in swap + [q for l in plane + depth + spread for q in l]:
        q.wait_send()
    for q in over:
        q.wait()


def dot(a,b,ca=1,cb=0):
    return lax.dot_general(a,b,(((ca,),(cb,)),((),())),precision=HI,preferred_element_type=jnp.float32)
def diag_block(w):
    lane=lax.broadcasted_iota(jnp.int32,(8,128),1)
    sub=lax.broadcasted_iota(jnp.int32,(8,128),0)
    spread=lambda v,r:jnp.broadcast_to(v[r:r+1,:],(8,128))
    def gather(v,base,r):
        return jnp.take_along_axis(v,jnp.full((8,128),jnp.clip(base+r,0,127),jnp.int32),axis=1)
    def total(t):
        return ((t[0]+t[1])+(t[2]+t[3]))+((t[4]+t[5])+(t[6]+t[7]))
    def apply(A,C,W,base):
        group=(lane>=base)&(lane<base+8)
        return jnp.where(group,0.0,A)-total([C[r]*W[r] for r in range(8)])
    rowf=lax.broadcasted_iota(jnp.int32,(128,128),0)
    def make(lo):
      def step(p,carry):
        R,Q,Wp=carry
        base=pl.multiple_of(8*p,8)
        prev=base-8
        B=[gather(R,base,c) for c in range(8)]
        C=[gather(Q,base,r) for r in range(8)]
        S=w[pl.ds(base+16,8),:]
        G1=[gather(S,prev,r) for r in range(8)]
        Wl=[spread(Wp,r) for r in range(8)]
        S=apply(S,G1,Wl,prev)
        G2=[gather(S,base,r) for r in range(8)]
        A=w[8*lo:128,:]
        rowi=lax.broadcasted_iota(jnp.int32,A.shape,0)+8*lo
        lan=lax.broadcasted_iota(jnp.int32,A.shape,1)
        full=jnp.where((rowf>=prev)&(rowf<base),jnp.concatenate([Wp]*16,axis=0),0.0)
        N=jnp.where((lan>=prev)&(lan<base),0.0,A)-dot(A,full)
        w[8*lo:128,:]=jnp.where(rowi>=8*p+24,N,A)
        kept=R
        for r in range(8):
            here=sub==r
            row=spread(R,r)
            kept=jnp.where(here,row,kept)
            inv=1.0/spread(B[r],r)
            m=B[r]*inv
            for c in range(r+1,8):
                rc=spread(B[c],r)
                B[c]=jnp.where(here,rc*inv,B[c]-m*rc)
            hit=lane==base+r
            row=jnp.where(hit,1.0,row)
            R=jnp.where(here,row*inv,jnp.where(hit,0.0,R)-m*row)
        W=[spread(R,r) for r in range(8)]
        newR=apply(Q,C,W,base)
        newQ=apply(S,G2,W,base)
        w[pl.ds(base,8),:]=kept
        return newR,newQ,R
      return step
    carry=(w[0:8,:],w[8:16,:],jnp.zeros((8,128),jnp.float32))
    carry=lax.fori_loop(0,8,make(3),carry)
    lax.fori_loop(8,16,make(11),carry)
def factor_solve_scatter(
    g_ref, hi_ref, lo_ref, l_ref, o_ref, a_ref, li_ref, w, buf, relay, sa, ra, sb, rb, ls
):
    me, g = lax.axis_index("fibre"), lax.axis_index("group")
    x, y, c = me // 8, (me // 2) % 4, me % 2
    bar = pltpu.get_barrier_semaphore()
    targets = cross(me)
    for t in targets:
        pl.semaphore_signal(bar, inc=1, device_id=(t, g), device_id_type=MESH)

    def first(h, d, e):
        X, Y = (x + d, y + e) if h == 0 else (x + e, y + d)
        to = chip(x + d, y, c) if h == 0 else chip(x, y + d, c)
        return pltpu.make_async_remote_copy(
            src_ref=buf.at[h, rows((X % 4) * 4 + Y % 4, 16), :],
            dst_ref=relay.at[h, d, e],
            send_sem=sa.at[h, d, e],
            recv_sem=ra.at[h, d, e],
            device_id=(to, g),
            device_id_type=MESH,
        )

    def place(h, d, e, dc):
        X, Y = (x, y + e) if h == 0 else (x + e, y)
        C = (c + dc) % 2
        if d == 0:
            src, f = buf.at[h, rows(((X % 4) * 4 + Y % 4) * 2 + C, 8), :], me
        else:
            src = relay.at[h, d, e, rows(C, 8), :]
            f = chip(x - d + 4, y, c) if h == 0 else chip(x, y - d + 4, c)
        return src, o_ref.at[8 * h : 8 * h + 8, lanes(f, W)], (chip(X, Y, C), g)

    def last(h, d, e, dc):
        src, dst, to = place(h, d, e, dc)
        return pltpu.make_async_remote_copy(
            src_ref=src, dst_ref=dst, send_sem=sb.at[h, d, e, dc], recv_sem=rb.at[h, d, e, dc],
            device_id=to, device_id_type=MESH,
        )

    def stay(h, d, e):
        src, dst, to = place(h, d, e, 0)
        return pltpu.make_async_copy(src, dst, ls.at[h, d])

    def go(h, d, e):
        last(h, d, e, 1).start()
        if h == 0:
            if e == 0:
                stay(h, d, e).start()
            else:
                last(h, d, e, 0).start()
        else:
            pl.when(e == 0)(lambda: stay(h, d, e).start())
            pl.when(e != 0)(lambda: last(h, d, e, 0).start())

    def post(k):
        off = (k - x + 4) % 4

        @pl.when(off != 0)
        def _():
            for e in (2, 1, 3, 0):
                first(0, off, e).start()

        @pl.when(off == 0)
        def _():
            for e in (2, 1, 3, 0):
                go(0, 0, e)

        for d in (2, 1, 3):
            first(1, d, off).start()
        go(1, 0, off)

    def forward(k):
        off = (k - x + 4) % 4
        for d in (2, 1, 3):
            first(1, d, off).wait_recv()
            go(1, d, off)

        @pl.when(off == 0)
        def _():
            for d in (2, 1, 3):
                for e in (2, 1, 3, 0):
                    first(0, d, e).wait_recv()
                    go(0, d, e)

    l_ref[...] = jnp.zeros((M, M), jnp.float32)
    li_ref[...] = jnp.zeros((M, M), jnp.float32)
    B = 128
    for i in range(4):
        for j in range(i + 1):
            b = i * (i + 1) // 2 + j
            a_ref[B * i : B * i + B, B * j : B * j + B] = g_ref[B * b : B * b + B, :]
    ri = lax.broadcasted_iota(jnp.int32, (B, B), 0)
    ci = lax.broadcasted_iota(jnp.int32, (B, B), 1)
    for k in range(4):
        o, n = k * B, (k + 1) * B
        w[0:B, :] = a_ref[o:n, o:n]
        diag_block(w)
        A = w[0:B, :]
        rs = lax.rsqrt(jnp.sum(jnp.where(ri == ci, A, 0.0), axis=1, keepdims=True))
        U = jnp.where(ci >= ri, A, 0.0) * rs
        LI = jnp.where(ci < ri, A, jnp.where(ri == ci, 1.0, 0.0)) * rs
        l_ref[o:n, o:n] = U.T
        if k:
            li_ref[o:n, 0:o] = -dot(LI, dot(l_ref[o:n, 0:o], li_ref[0:o, 0:o]))
        li_ref[o:n, o:n] = LI
        li = li_ref[o:n, 0:n].reshape(8, 2, 8, n)
        li = jnp.concatenate([li[:, 0].reshape(64, n), li[:, 1].reshape(64, n)], axis=0)
        lh = li.astype(jnp.bfloat16)
        ll = (li - lh.astype(jnp.float32)).astype(jnp.bfloat16)
        hi = hi_ref[0:n, :]
        X = bdot(lh, hi, 1, 0) + (bdot(lh, lo_ref[0:n, :], 1, 0) + bdot(ll, hi, 1, 0))
        buf[0, 64 * k : 64 * k + 64, :] = X[0:64]
        buf[1, 64 * k : 64 * k + 64, :] = X[64:128]
        if k == 0:
            pl.semaphore_wait(bar, len(targets))
        post(k)
        if k >= 2:
            forward(k - 2)
        if k < 3:
            L21 = dot(a_ref[n:, o:n], LI, 1, 1)
            l_ref[n:, o:n] = L21
            a_ref[n:, n:] = a_ref[n:, n:] - dot(L21, L21, 1, 1)
    forward(2)
    forward(3)
    for h in range(2):
        for d in range(4):
            for e in range(4):
                if d:
                    first(h, d, e).wait_send()
                last(h, d, e, 1).wait()
                if e:
                    last(h, d, e, 0).wait()
            stay(h, d, 0).wait()


def local(tensor):
    f32, bf16, shape = jnp.float32, jnp.bfloat16, jax.ShapeDtypeStruct
    hops = [
        pltpu.SemaphoreType.DMA(n)
        for n in ((2, 4, 4), (2, 4, 4), (2, 4, 4, 2), (2, 4, 4, 2), (2, 4))
    ]
    vmem, dma = pl.BlockSpec(memory_space=pltpu.VMEM), pltpu.SemaphoreType.DMA
    hi, lo, gram = pl.pallas_call(
        gather_gram,
        out_shape=(shape((M, W), bf16), shape((M, W), bf16), shape((PACK, 128), f32)),
        in_specs=[pl.BlockSpec(memory_space=pl.ANY)],
        out_specs=(vmem, vmem, vmem),
        scratch_shapes=[
            pltpu.VMEM((M, W), f32),
            pltpu.VMEM((2, 3, 4, 8, 2 * W), f32),
            pltpu.VMEM((PACK, 128), f32),
            pltpu.VMEM((HALF, 128), f32),
            pltpu.VMEM((HALF, 128), f32),
            pltpu.VMEM((NF // 2, OWN, 128), f32),
            pltpu.VMEM((OWN, 128), f32),
            pltpu.VMEM((NG, OWN, 128), f32),
            *hops,
            dma((2,)),
            dma((2,)),
            dma((30,)),
            dma((30,)),
            dma((14,)),
            dma((14,)),
            dma((30,)),
            dma((30,)),
            dma((32,)),
            dma((32,)),
        ],
        compiler_params=pltpu.CompilerParams(collective_id=0, has_side_effects=True, vmem_limit_bytes=32 << 20),
    )(tensor)
    factor, basis = pl.pallas_call(
        factor_solve_scatter,
        out_shape=(shape((M, M), f32), shape(tensor.shape, f32)),
        in_specs=[vmem] * 3,
        out_specs=(vmem, pl.BlockSpec(memory_space=pl.ANY)),
        scratch_shapes=[
            pltpu.VMEM((M, M), f32),
            pltpu.VMEM((M, M), f32),
            pltpu.VMEM((144, 128), f32),
            pltpu.VMEM((2, M // 2, W), f32),
            pltpu.VMEM((2, 4, 4, 16, W), f32),
            *hops,
        ],
        compiler_params=pltpu.CompilerParams(collective_id=1, has_side_effects=True, vmem_limit_bytes=32 << 20),
    )(gram, hi, lo)
    return basis, factor


def solution(mesh):
    return jax.shard_map(
        local,
        mesh=mesh,
        in_specs=(P("fibre", "group"),),
        out_specs=(P("fibre", "group"), P()),
        check_vma=False,
    )
```

time: 487 us -> 138 us (0.28); the launches traced: 478 us -> 138 us
  waiting for transfers between devices: 204 us -> 0 us
  Pallas kernels: 0 us -> 133 us
  other arithmetic: 124 us -> 0 us
  blocking collectives: 92.6 us -> 0 us
  matrix products: 20 us -> 0 us
  starting transfers between devices: 14.7 us -> 0 us
  local copies, waits for them, and re-layouts: 18.7 us -> 4.52 us
    ppermute x8 -> x0, waiting for transfers between devices: 204 us -> none  [partner_2(): lax.ppermute(x, axis, [(i, i ^ 1 << bit) for i in range(lax.axis_size(axi...]
    pallas_call x0 -> x2, Pallas kernels: none -> 133 us  [the longest x1 73.6 us: local(): pl.pallas_call(gather_gram, out_shape=(shape((M, W), bf16), shape((M, W),...]
    another operation x18 -> x0, other arithmetic: 120 us -> none  [the longest x14 78.8 us: local(): factor = jnp.linalg.cholesky(summed)]
    all_to_all x2 -> x0, blocking collectives: 92.6 us -> none  [the longest x1 47.8 us: local(): lax.all_to_all(tensor, 'fibre', split_axis=1, concat_axis=0, tiled=True)]
    another operation x13 -> x0, matrix products: 14.9 us -> none  [the longest x7 9.39 us: local(): lax.linalg.triangular_solve(factor, columns, left_side=True, lower=True)]
    ppermute x8 -> x0, starting transfers between devices: 14.7 us -> none  [partner_2(): lax.ppermute(x, axis, [(i, i ^ 1 << bit) for i in range(lax.axis_size(axi...]
    another operation x18 -> x0, local copies, waits for them, and re-layouts: 13.5 us -> none
    dot_general x1 -> x0, matrix products: 5.12 us -> none  [local(): jnp.dot(columns, columns.T, precision=lax.Precision.HIGHEST, preferred_el...]
  transfers between devices with their start and end apart: 8 -> 0, of which waited for: 8 -> 0; matrix products, arithmetic and copies ran while one was open for 0% -> 0% of each run, Pallas kernels for 0% -> 0%
where the time goes in v2:
time: 138 us
  Pallas kernels  133 us (96%)
  local copies, waits for them, and re-layouts  4.52 us (3%)
    pallas_call x1, Pallas kernels, local(): pl.pallas_call(gather_gram, out_shape=(shape((M, W), bf16), shape((M, W),...  73.6 us
    pallas_call x1, Pallas kernels, local(): pl.pallas_call(factor_solve_scatter, out_shape=(shape((M, M), f32), shape...  59.3 us
    unnamed x4, local copies, waits for them, and re-layouts  4.52 us

profile of v2, /device:TPU:1, one launch (start us, length us, event | category | flops | bytes accessed | tf_op | source)
XLA Modules:
  0.0 138.1 jit_solution(9152561062059491804)
XLA Ops:
  0.6 0.0 copy-start
  0.6 1.9 %copy-done = f32[16,49152]{1,0:T(8,128)S(1)} copy-done((f32[16,49152]{1,0:T(8,128)S(1)}, f32[16,49152]{1,0:T(8,128)}, u32[]{:S(2)}) %copy-start) | copy-done | bytes 3145752
  2.5 73.6 %shard_map.30 = (bf16[512,1536]{1,0:T(8,128)(2,1)S(1)}, bf16[512,1536]{1,0:T(8,128)(2,1)S(1)}, f32[1280,128]{1,0:T(8,128)S(1)}) custom-call(f32[16,49152]{1,0:T(8,128)S(1)} %copy-done), custom_call_target="tpu_custom_call" | custom-call | tf_op jit(solution)/shard_map/pallas_call | solution.py:413
  76.1 59.3 %shard_map.31 = (f32[512,512]{1,0:T(8,128)S(1)}, f32[16,49152]{1,0:T(8,128)S(1)}) custom-call(f32[1280,128]{1,0:T(8,128)S(1)} %get-tuple-element.7.g_ref, bf16[512,1536]{1,0:T(8,128)(2,1)S(1)} %get-tuple-element.8.hi_ref, bf16[512,1536]{1,0:T(8,128)(2,1)S(1)} %get-tuple-element.9.lo_ref), custom_call_target="tpu_custom_call" | custom-call | tf_op jit(solution)/shard_map/pallas_call | solution.py:441
  135.4 1.7 %copy.5 = f32[16,49152]{1,0:T(8,128)} copy(f32[16,49152]{1,0:T(8,128)S(1)} %get-tuple-element.14) | data formatting | bytes 6291456
  137.1 1.0 copy.6
Async XLA Ops:
  0.6 1.9 %copy-start = (f32[16,49152]{1,0:T(8,128)S(1)}, f32[16,49152]{1,0:T(8,128)}, u32[]{:S(2)}) copy-start(f32[16,49152]{1,0:T(8,128)} %x_ref.1) | copy-start | bytes 9437188

commit v3 on v2

--- a/solution.py
+++ b/solution.py
@@ -137,14 +137,16 @@
         top = v.astype(jnp.bfloat16)
         hi_ref[128 * k : 128 * k + 128, :] = top
         lo_ref[128 * k : 128 * k + 128, :] = (v - top.astype(jnp.float32)).astype(jnp.bfloat16)
-    for i in range(4):
-        a, al = hi_ref[128 * i : 128 * i + 128, :], lo_ref[128 * i : 128 * i + 128, :]
-        n = 128 * (i + 1)
-        b, bl = hi_ref[0:n, :], lo_ref[0:n, :]
-        blk = (bdot(a, b, 1, 1) + (bdot(a, bl, 1, 1) + bdot(al, b, 1, 1))) * (1.0 / COLS)
-        for j in range(i + 1):
-            o = 128 * (i * (i + 1) // 2 + j)
-            part[o : o + 128, :] = blk[:, 128 * j : 128 * j + 128]
+    for i in range(2):
+        n = 256 * (i + 1)
+        a = hi_ref[n - 256 : n, :]
+        both = jnp.concatenate([a, lo_ref[n - 256 : n, :]], axis=0)
+        top = bdot(both, hi_ref[0:n, :], 1, 1)
+        blk = (top[0:256] + (top[256:512] + bdot(a, lo_ref[0:n, :], 1, 1))) * (1.0 / COLS)
+        for r in range(2):
+            for j in range(2 * i + r + 1):
+                o = 128 * ((2 * i + r) * (2 * i + r + 1) // 2 + j)
+                part[o : o + 128, :] = blk[128 * r : 128 * r + 128, 128 * j : 128 * j + 128]
 
     x, y, c = me // 8, (me // 2) % 4, me % 2
     p, twin = me // 2, (chip(x, y, c + 1), g)
@@ -339,18 +341,17 @@
             first(1, d, off).start()
         go(1, 0, off)
 
-    def forward(k):
+    def turn_x(k):
         off = (k - x + 4) % 4
         for d in (2, 1, 3):
             first(1, d, off).wait_recv()
             go(1, d, off)
 
-        @pl.when(off == 0)
-        def _():
-            for d in (2, 1, 3):
-                for e in (2, 1, 3, 0):
-                    first(0, d, e).wait_recv()
-                    go(0, d, e)
+    def turn_y():
+        for d in (2, 1, 3):
+            for e in (2, 1, 3, 0):
+                first(0, d, e).wait_recv()
+                go(0, d, e)
 
     l_ref[...] = jnp.zeros((M, M), jnp.float32)
     li_ref[...] = jnp.zeros((M, M), jnp.float32)
@@ -377,21 +378,23 @@
         li = jnp.concatenate([li[:, 0].reshape(64, n), li[:, 1].reshape(64, n)], axis=0)
         lh = li.astype(jnp.bfloat16)
         ll = (li - lh.astype(jnp.float32)).astype(jnp.bfloat16)
-        hi = hi_ref[0:n, :]
-        X = bdot(lh, hi, 1, 0) + (bdot(lh, lo_ref[0:n, :], 1, 0) + bdot(ll, hi, 1, 0))
+        top = bdot(jnp.concatenate([lh, ll], axis=0), hi_ref[0:n, :], 1, 0)
+        X = top[0:128] + (top[128:256] + bdot(lh, lo_ref[0:n, :], 1, 0))
         buf[0, 64 * k : 64 * k + 64, :] = X[0:64]
         buf[1, 64 * k : 64 * k + 64, :] = X[64:128]
         if k == 0:
             pl.semaphore_wait(bar, len(targets))
         post(k)
         if k >= 2:
-            forward(k - 2)
+            turn_x(k - 2)
         if k < 3:
             L21 = dot(a_ref[n:, o:n], LI, 1, 1)
             l_ref[n:, o:n] = L21
             a_ref[n:, n:] = a_ref[n:, n:] - dot(L21, L21, 1, 1)
-    forward(2)
-    forward(3)
+    turn_x(2)
+    pl.when(x == 0)(turn_y)
+    turn_x(3)
+    pl.when(x != 0)(turn_y)
     for h in range(2):
         for d in range(4):
             for e in range(4):

time: 138 us -> 137 us (level)
  Pallas kernels: 133 us -> 131 us
    pallas_call x1, Pallas kernels: 73.6 us -> 71.9 us  [local(): pl.pallas_call(gather_gram, out_shape=(shape((M, W), bf16), shape((M, W),...]
where the time goes in v3:
time: 137 us; the launch traced here: 136 us
  Pallas kernels  131 us (96%)
  local copies, waits for them, and re-layouts  4.52 us (3%)
    pallas_call x1, Pallas kernels, local(): pl.pallas_call(gather_gram, out_shape=(shape((M, W), bf16), shape((M, W),...  71.9 us
    pallas_call x1, Pallas kernels, local(): pl.pallas_call(factor_solve_scatter, out_shape=(shape((M, M), f32), shape...  59.3 us
    unnamed x4, local copies, waits for them, and re-layouts  4.52 us

profile of v3, /device:TPU:1, one launch (start us, length us, event | category | flops | bytes accessed | tf_op | source)
XLA Modules:
  0.0 136.4 jit_solution(9759979038814231820)
XLA Ops:
  0.6 0.0 copy-start
  0.6 1.9 %copy-done = f32[16,49152]{1,0:T(8,128)S(1)} copy-done((f32[16,49152]{1,0:T(8,128)S(1)}, f32[16,49152]{1,0:T(8,128)}, u32[]{:S(2)}) %copy-start) | copy-done | bytes 3145752
  2.5 71.9 %shard_map.30 = (bf16[512,1536]{1,0:T(8,128)(2,1)S(1)}, bf16[512,1536]{1,0:T(8,128)(2,1)S(1)}, f32[1280,128]{1,0:T(8,128)S(1)}) custom-call(f32[16,49152]{1,0:T(8,128)S(1)} %copy-done), custom_call_target="tpu_custom_call" | custom-call | tf_op jit(solution)/shard_map/pallas_call | solution.py:416
  74.5 59.3 %shard_map.31 = (f32[512,512]{1,0:T(8,128)S(1)}, f32[16,49152]{1,0:T(8,128)S(1)}) custom-call(f32[1280,128]{1,0:T(8,128)S(1)} %get-tuple-element.7.g_ref, bf16[512,1536]{1,0:T(8,128)(2,1)S(1)} %get-tuple-element.8.hi_ref, bf16[512,1536]{1,0:T(8,128)(2,1)S(1)} %get-tuple-element.9.lo_ref), custom_call_target="tpu_custom_call" | custom-call | tf_op jit(solution)/shard_map/pallas_call | solution.py:444
  133.7 1.7 %copy.5 = f32[16,49152]{1,0:T(8,128)} copy(f32[16,49152]{1,0:T(8,128)S(1)} %get-tuple-element.14) | data formatting | bytes 6291456
  135.4 1.0 copy.6
Async XLA Ops:
  0.6 1.9 %copy-start = (f32[16,49152]{1,0:T(8,128)S(1)}, f32[16,49152]{1,0:T(8,128)}, u32[]{:S(2)}) copy-start(f32[16,49152]{1,0:T(8,128)} %x_ref.1) | copy-start | bytes 9437188

commit v4 on v3

--- a/solution.py
+++ b/solution.py
@@ -416,7 +416,7 @@
     hi, lo, gram = pl.pallas_call(
         gather_gram,
         out_shape=(shape((M, W), bf16), shape((M, W), bf16), shape((PACK, 128), f32)),
-        in_specs=[pl.BlockSpec(memory_space=pl.ANY)],
+        in_specs=[pl.BlockSpec(memory_space=pltpu.HBM)],
         out_specs=(vmem, vmem, vmem),
         scratch_shapes=[
             pltpu.VMEM((M, W), f32),
@@ -440,7 +440,7 @@
             dma((32,)),
         ],
         compiler_params=pltpu.CompilerParams(collective_id=0, has_side_effects=True, vmem_limit_bytes=32 << 20),
-    )(tensor)
+    )(pltpu.with_memory_space_constraint(tensor, pltpu.HBM))
     factor, basis = pl.pallas_call(
         factor_solve_scatter,
         out_shape=(shape((M, M), f32), shape(tensor.shape, f32)),

time: 137 us -> 135 us (0.985)
  local copies, waits for them, and re-layouts: 4.52 us -> 2.64 us
    unnamed x4 -> x2, local copies, waits for them, and re-layouts: 4.52 us -> 2.64 us
where the time goes in v4:
time: 135 us
  Pallas kernels  132 us (98%)
  local copies, waits for them, and re-layouts  2.64 us (2%)
    pallas_call x1, Pallas kernels, local(): pl.pallas_call(gather_gram, out_shape=(shape((M, W), bf16), shape((M, W),...  72.4 us
    pallas_call x1, Pallas kernels, local(): pl.pallas_call(factor_solve_scatter, out_shape=(shape((M, M), f32), shape...  59.3 us

profile of v4, /device:TPU:1, one launch (start us, length us, event | category | flops | bytes accessed | tf_op | source)
XLA Modules:
  0.0 135.0 jit_solution(4616018618951435293)
XLA Ops:
  0.6 72.4 %shard_map.30 = (bf16[512,1536]{1,0:T(8,128)(2,1)S(1)}, bf16[512,1536]{1,0:T(8,128)(2,1)S(1)}, f32[1280,128]{1,0:T(8,128)S(1)}) custom-call(f32[16,49152]{1,0:T(8,128)} %x_ref.1), custom_call_target="tpu_custom_call" | custom-call | tf_op jit(solution)/shard_map/pallas_call | solution.py:416
  73.0 59.3 %shard_map.31 = (f32[512,512]{1,0:T(8,128)S(1)}, f32[16,49152]{1,0:T(8,128)S(1)}) custom-call(f32[1280,128]{1,0:T(8,128)S(1)} %get-tuple-element.7.g_ref, bf16[512,1536]{1,0:T(8,128)(2,1)S(1)} %get-tuple-element.8.hi_ref, bf16[512,1536]{1,0:T(8,128)(2,1)S(1)} %get-tuple-element.9.lo_ref), custom_call_target="tpu_custom_call" | custom-call | tf_op jit(solution)/shard_map/pallas_call | solution.py:444
  132.3 1.7 %copy.5 = f32[16,49152]{1,0:T(8,128)} copy(f32[16,49152]{1,0:T(8,128)S(1)} %get-tuple-element.14) | data formatting | bytes 6291456
  134.0 1.0 copy.6
